TPU v7x, 32 devices: a whole 2x2x4 slice. The times are simulated.
32 devices in a mesh: dp: 4 (over y, x), seq: 8 (over z, core).
Axes of the slice: x: 2, y: 2, z: 4, core: 2. Of those that a mesh axis runs over, the one named last changes fastest.
Arguments:
- tiles: bfloat16 [4, 8192, 768], P('dp', 'seq'), may hold values from -48 to 48
- tile_count: int32 [4], P('dp'), may hold values from 4097 to 8192
- offsets: int32 [16], replicated, may hold values from 0 to 15
- w_query: bfloat16 [768, 768], replicated, may hold values from -0.375 to 0.375
- w_key: bfloat16 [768, 768], replicated, may hold values from -0.375 to 0.375
- w_value: bfloat16 [768, 768], replicated, may hold values from -0.21875 to 0.21875
- w_out: bfloat16 [768, 768], replicated, may hold values from -0.21875 to 0.21875
- cotangent: bfloat16 [4, 8192, 768], P('dp', 'seq'), may hold values from -0.046875 to 0.046875
Outputs:
- branch: bfloat16 [4, 8192, 768], P('dp', 'seq')
- grad_out: float32 [768, 768], P(None, 'seq')
All inputs are finite; a program needn't handle non-finite values.
Results may differ from a plain program's by a relative error of at most 0.0095.
The roundings to bfloat16 on the way count: a program that leaves them out, or rounds other values in their place, can miss the bound.
Values may be sent and summed in bfloat16 or wider, within the bound.
A program may use at most 128 MiB of HBM per device.

v0:
```python
import jax
import jax.numpy as jnp
from jax import lax
from jax.sharding import PartitionSpec as P

D = 768
ATTENTION_HEADS = 16
HEAD_SIZE = 48
SEG = 1024
RATE = 16
NEGATIVE_FLOOR = -1e30
head_group = 4


def project(inputs, weight):
    return jnp.dot(inputs, weight, preferred_element_type=jnp.float32).astype(jnp.bfloat16)


def select_rows(tensor, offsets):
    segment_height = tensor.shape[0]
    grouped = tensor.reshape(segment_height // RATE, RATE, ATTENTION_HEADS, HEAD_SIZE)
    onehot = (jnp.arange(RATE, dtype=jnp.int32)[:, None] == offsets[None, :]).astype(jnp.bfloat16)
    return jnp.einsum("arhd,rh->ahd", grouped, onehot, preferred_element_type=jnp.float32).astype(
        jnp.bfloat16
    )


def local_attention(query_proj, key_proj, value_proj, is_live):
    segment_height = query_proj.shape[0]
    segments = segment_height // SEG
    groups = ATTENTION_HEADS // head_group
    query_seg = query_proj.reshape(segments, SEG, groups, head_group, HEAD_SIZE)
    key_seg = key_proj.reshape(segments, SEG, groups, head_group, HEAD_SIZE)
    value_seg = value_proj.reshape(segments, SEG, groups, head_group, HEAD_SIZE)
    alive_seg = is_live.reshape(segments, SEG)

    def one_group(index):
        query_part = lax.dynamic_index_in_dim(query_seg, index, 2, keepdims=False)
        key_part = lax.dynamic_index_in_dim(key_seg, index, 2, keepdims=False)
        value_part = lax.dynamic_index_in_dim(value_seg, index, 2, keepdims=False)
        scores = jnp.einsum(
            "sqhd,skhd->shqk", query_part, key_part, preferred_element_type=jnp.float32
        ) * HEAD_SIZE ** (-0.5)
        scores = jnp.where(alive_seg[:, None, None, :], scores, NEGATIVE_FLOOR)
        maxima = jnp.max(scores, axis=-1)
        weights = jnp.exp(scores - maxima[..., None])
        totals = jnp.sum(weights, axis=-1)
        weighted = jnp.einsum(
            "shqk,skhd->sqhd",
            weights.astype(jnp.bfloat16),
            value_part,
            preferred_element_type=jnp.float32,
        )
        return (maxima, totals, weighted)

    maxima, totals, weighted = lax.map(one_group, jnp.arange(groups, dtype=jnp.int32))
    maxima = maxima.transpose(1, 3, 0, 2).reshape(segment_height, ATTENTION_HEADS)
    totals = totals.transpose(1, 3, 0, 2).reshape(segment_height, ATTENTION_HEADS)
    weighted = weighted.transpose(1, 2, 0, 3, 4).reshape(segment_height, ATTENTION_HEADS, HEAD_SIZE)
    return (maxima, totals, weighted)


def combine(local, dilated_branch, offsets, is_live):
    local_max, local_total, local_sum = local
    dilated_row_max, dilated_value_total, dilated_row_sum = dilated_branch
    segment_height = local_max.shape[0]
    dilation_match = jnp.arange(RATE, dtype=jnp.int32)[:, None] == offsets[None, :]
    dense_row_max = jnp.where(
        dilation_match[None], dilated_row_max[:, None, :], NEGATIVE_FLOOR
    ).reshape(segment_height, ATTENTION_HEADS)
    dense_value_total = jnp.where(
        dilation_match[None], dilated_value_total[:, None, :], 0.0
    ).reshape(segment_height, ATTENTION_HEADS)
    dense_row_sum = jnp.where(
        dilation_match[None, :, :, None], dilated_row_sum[:, None], 0.0
    ).reshape(segment_height, ATTENTION_HEADS, HEAD_SIZE)
    top = jnp.maximum(local_max, dense_row_max)
    near = jnp.exp(local_max - top)
    far = jnp.exp(dense_row_max - top)
    attn = (near[..., None] * local_sum + far[..., None] * dense_row_sum) / (
        near * local_total + far * dense_value_total
    )[..., None]
    attn = jnp.where(is_live[:, None, None], attn, 0.0)
    return attn.reshape(segment_height, D).astype(jnp.bfloat16)


def body(tiles, tile_count, offsets, w_query, w_key, w_value, w_out, cotangent):
    inputs = tiles[0]
    segment_height = inputs.shape[0]
    shard_rank = lax.axis_index("seq")
    live_count = tile_count[0]
    query_proj = project(inputs, w_query).reshape(segment_height, ATTENTION_HEADS, HEAD_SIZE)
    key_proj = project(inputs, w_key).reshape(segment_height, ATTENTION_HEADS, HEAD_SIZE)
    value_proj = project(inputs, w_value).reshape(segment_height, ATTENTION_HEADS, HEAD_SIZE)
    positions = shard_rank * segment_height + jnp.arange(segment_height, dtype=jnp.int32)
    is_live = positions < live_count
    local = local_attention(query_proj, key_proj, value_proj, is_live)
    picked = segment_height // RATE
    query_sel = select_rows(query_proj, offsets)
    key_sel = select_rows(key_proj, offsets)
    value_sel = select_rows(value_proj, offsets)
    score_scale = HEAD_SIZE ** (-0.5)
    portion = (
        lax.all_gather(key_sel.reshape(picked, D), "seq", axis=0, tiled=True),
        lax.all_gather(value_sel.reshape(picked, D), "seq", axis=0, tiled=True),
    )
    old_max = jnp.full((picked, ATTENTION_HEADS), NEGATIVE_FLOOR, jnp.float32)
    key_part = portion[0].reshape(portion[0].shape[0], ATTENTION_HEADS, HEAD_SIZE)
    value_part = portion[1].reshape(portion[1].shape[0], ATTENTION_HEADS, HEAD_SIZE)
    amount = key_part.shape[0]
    key_live = jnp.arange(amount, dtype=jnp.int32)[:, None] * RATE + offsets[None, :] < live_count
    scores = (
        jnp.einsum("qhd,khd->qhk", query_sel, key_part, preferred_element_type=jnp.float32)
        * score_scale
    )
    scores = jnp.where(key_live.T[None], scores, NEGATIVE_FLOOR)
    new_max = jnp.maximum(old_max, jnp.max(scores, axis=-1))
    weights = jnp.exp(scores - new_max[..., None])
    new_total = jnp.sum(weights, axis=-1)
    new_sum = jnp.einsum(
        "qhk,khd->qhd", weights.astype(jnp.bfloat16), value_part, preferred_element_type=jnp.float32
    )
    dilated_branch = (new_max, new_total, new_sum)
    attn = combine(local, dilated_branch, offsets, is_live)
    branch = jnp.dot(attn, w_out, preferred_element_type=jnp.float32).astype(jnp.bfloat16)[None]
    gradient_in = cotangent[0]
    shares = lax.psum_scatter(
        jnp.einsum("tc,td->cd", gradient_in, attn, preferred_element_type=jnp.float32),
        "seq",
        scatter_dimension=0,
        tiled=True,
    )
    grad_part = lax.psum(shares.astype(jnp.bfloat16), "dp").astype(jnp.float32).T
    return (branch, grad_part)


def solution(mesh):
    in_specs = (P("dp", "seq", None), P("dp"), P(), P(), P(), P(), P(), P("dp", "seq", None))
    out_specs = (P("dp", "seq", None), P(None, "seq"))
    return jax.shard_map(body, mesh=mesh, in_specs=in_specs, out_specs=out_specs, check_vma=False)
```

profile of v0, /device:TPU:0, one launch (start us, length us, event | category | flops | bytes accessed | tf_op | source)
XLA Modules:
  0.0 290.6 jit_solution(8163011718679875207)
XLA Ops:
  7.2 0.6 iota_multiply_fusion
  8.5 0.7 iota_compare_fusion
  9.7 2.8 convolution_convert_fusion.3
  12.5 2.6 convolution_convert_fusion.2
  15.1 2.6 convolution_convert_fusion.1
  17.7 2.8 copy.49
  20.4 1.6 copy.45
  22.1 1.6 copy.47
  23.6 7.2 %reshape_reshape.22 = bf16[64,16,16,48]{3,2,1,0:T(8,128)(2,1)} reshape(bf16[1024,768]{1,0:T(8,128)(2,1)} %copy.47) | data formatting | bytes 3145728 | tf_op jit(solution)/shard_map/reshape;reshape | solution.py:21
  30.8 7.2 %reshape_reshape.21 = bf16[64,16,16,48]{3,2,1,0:T(8,128)(2,1)} reshape(bf16[1024,768]{1,0:T(8,128)(2,1)} %copy.45) | data formatting | bytes 3145728 | tf_op jit(solution)/shard_map/reshape;reshape | solution.py:21
  38.0 7.2 %reshape_reshape.23 = bf16[64,16,16,48]{3,2,1,0:T(8,128)(2,1)} reshape(bf16[1024,768]{1,0:T(8,128)(2,1)} %copy.49) | data formatting | bytes 3145728 | tf_op jit(solution)/shard_map/reshape;reshape | solution.py:21
  45.2 9.0 %multiply_reduce_fusion.1 = (bf16[16,64,48]{2,0,1:T(8,128)(2,1)S(1)}, bf16[16,64,48]{2,0,1:T(8,128)(2,1)}, bf16[16,64,48]{2,0,1:T(8,128)(2,1)}) fusion(f32[16,16]{0,1:T(8,128)S(1)} %copy.80, bf16[64,16,16,48]{3,2,1,0:T(8,128)(2,1)} %reshape_reshape.22, bf16[64,16,16,48]{3,2,1,0:T(8,128)(2,1)} %reshape_reshape.23, bf16[64,16,16,48]{3,2,1,0:T(8,128)(2,1)} %reshape_reshape.21), kind=kLoop, calls=%fused_computation.25 | loop fusion | flops 6930432 | bytes 5014528
  54.1 0.9 copy.70
  55.1 1.2 reshape.266
  56.3 1.2 reshape.263
  57.5 18.4 %all_gather.6 = bf16[512,768]{1,0:T(8,128)(2,1)} all-gather(bf16[64,768]{1,0:T(8,128)(2,1)S(1)} %reshape.263), channel_id=1, replica_groups=mesh['dp'=4,'seq'=8] {'seq'}, dimensions={0}, use_global_device_ids=true | all-gather | bytes 884736 | tf_op jit(solution)/shard_map/all_gather | solution.py:104
  76.0 2.3 copy.46
  78.3 16.6 %all_gather.7 = bf16[512,768]{1,0:T(8,128)(2,1)} all-gather(bf16[64,768]{1,0:T(8,128)(2,1)S(1)} %reshape.266), channel_id=1, replica_groups=mesh['dp'=4,'seq'=8] {'seq'}, dimensions={0}, use_global_device_ids=true | all-gather | bytes 884736 | tf_op jit(solution)/shard_map/all_gather | solution.py:105
  94.9 2.3 copy.50
  97.3 1.8 bitcast_reduce_fusion
  99.1 1.4 fusion.34
  100.5 0.6 convolution_bitcast_fusion.1
  101.1 1.0 copy.51
  102.1 1.7 broadcast_in_dim.151
  103.8 1.3 broadcast_in_dim.152
  105.1 1.7 broadcast_in_dim.159
  106.8 1.3 broadcast_in_dim.160
  108.7 66.5 %while.15 = (s32[]{:T(128)}, f32[4,1,4,1024]{3,2,1,0:T(4,128)}, f32[4,1,4,1024]{3,2,1,0:T(4,128)}, f32[4,1,1024,4,48]{2,4,3,1,0:T(8,128)}, s32[4]{0:T(128)S(1)},...) while((s32[]{:T(128)}, f32[4,1,4,1024]{3,2,1,0:T(4,128)}, ...), condition=%wide.region_3.4_spmd.clone, body=%wide.region_0.3_spmd.clone.sunk | while | flops 851437568 | bytes 52434116 | solution.py:56
  108.7 0.6 dynamic_slice.41
  111.0 0.7 add_compare_fusion.4
  111.6 3.3 %fusion.70 = (f32[4,1024]{1,0:T(4,128)S(1)}, f32[4,1024,1024]{1,2,0:T(8,128)S(1)}) fusion(pred[1024]{0:T(1024)(128)(4,1)S(1)} %add_compare_fusion.4, bf16[1,1024,4,4,48]{1,4,3,2,0:T(8,128)(2,1)S(1)} %get-tuple-element.223, s32[]{:T(128)S(6)} %select_n.128, bf16[1,1024,4,4,48]{1,4,3,2,0:T(8,128)(2,1)S(1)} %get-tuple-element.222), kind=kOutput, calls=%fused_computation.3.clone.1 | convolution fusion | flops 415232000 | bytes 17582080 | tf_op jit(solution)/shard_map/while/body/eval_jaxpr/sqhd,skhd->shqk/dot_general | solution.py:41
  115.0 4.1 %fusion.71 = f32[4,1024]{1,0:T(4,128)S(1)} fusion(f32[4,1024,1024]{1,2,0:T(8,128)S(1)} %get-tuple-element.187, f32[4,1024]{1,0:T(4,128)S(1)} %get-tuple-element.188, pred[1024]{0:T(1024)(128)(4,1)S(1)} %add_compare_fusion.4), kind=kLoop, calls=%fused_computation.5.clone.1 | loop fusion | flops 16773120 | bytes 16811008 | tf_op jit(solution)/shard_map/while/body/eval_jaxpr/reduce_sum | solution.py:47
  119.1 5.7 %fusion.72 = f32[4,1,1024,4,48]{2,4,3,1,0:T(8,128)} fusion(f32[4,1,1024,4,48]{2,4,3,1,0:T(8,128)} %get-tuple-element.207, s32[]{:T(128)S(6)} %copy.89, f32[4,1024,1024]{1,2,0:T(8,128)S(1)} %get-tuple-element.187, f32[4,1024]{1,0:T(4,128)S(1)} %get-tuple-element.188, pred[1024]{0:T(1024)(128)(4,1)S(1)} %add_compare_fusion.4, ...), kind=kOutput, calls=%fused_computation.9.clone.1 | convolution fusion | flops 419430400 | bytes 17974280 | tf_op jit(solution)/shard_map/while/body/eval_jaxpr/shqk,skhd->sqhd/dot_general | solution.py:48
  124.8 0.6 bitcast_dynamic-update-slice_fusion.3
  127.6 0.7 add_compare_fusion.4
  128.3 3.3 %fusion.70 = (f32[4,1024]{1,0:T(4,128)S(1)}, f32[4,1024,1024]{1,2,0:T(8,128)S(1)}) fusion(pred[1024]{0:T(1024)(128)(4,1)S(1)} %add_compare_fusion.4, bf16[1,1024,4,4,48]{1,4,3,2,0:T(8,128)(2,1)S(1)} %get-tuple-element.223, s32[]{:T(128)S(6)} %select_n.128, bf16[1,1024,4,4,48]{1,4,3,2,0:T(8,128)(2,1)S(1)} %get-tuple-element.222), kind=kOutput, calls=%fused_computation.3.clone.1 | convolution fusion | flops 415232000 | bytes 17582080 | tf_op jit(solution)/shard_map/while/body/eval_jaxpr/sqhd,skhd->shqk/dot_general | solution.py:41
  131.6 4.1 %fusion.71 = f32[4,1024]{1,0:T(4,128)S(1)} fusion(f32[4,1024,1024]{1,2,0:T(8,128)S(1)} %get-tuple-element.187, f32[4,1024]{1,0:T(4,128)S(1)} %get-tuple-element.188, pred[1024]{0:T(1024)(128)(4,1)S(1)} %add_compare_fusion.4), kind=kLoop, calls=%fused_computation.5.clone.1 | loop fusion | flops 16773120 | bytes 16811008 | tf_op jit(solution)/shard_map/while/body/eval_jaxpr/reduce_sum | solution.py:47
  135.8 5.6 %fusion.72 = f32[4,1,1024,4,48]{2,4,3,1,0:T(8,128)} fusion(f32[4,1,1024,4,48]{2,4,3,1,0:T(8,128)} %get-tuple-element.207, s32[]{:T(128)S(6)} %copy.89, f32[4,1024,1024]{1,2,0:T(8,128)S(1)} %get-tuple-element.187, f32[4,1024]{1,0:T(4,128)S(1)} %get-tuple-element.188, pred[1024]{0:T(1024)(128)(4,1)S(1)} %add_compare_fusion.4, ...), kind=kOutput, calls=%fused_computation.9.clone.1 | convolution fusion | flops 419430400 | bytes 17974280 | tf_op jit(solution)/shard_map/while/body/eval_jaxpr/shqk,skhd->sqhd/dot_general | solution.py:48
  141.4 0.6 bitcast_dynamic-update-slice_fusion.3
  144.2 0.7 add_compare_fusion.4
  144.9 3.3 %fusion.70 = (f32[4,1024]{1,0:T(4,128)S(1)}, f32[4,1024,1024]{1,2,0:T(8,128)S(1)}) fusion(pred[1024]{0:T(1024)(128)(4,1)S(1)} %add_compare_fusion.4, bf16[1,1024,4,4,48]{1,4,3,2,0:T(8,128)(2,1)S(1)} %get-tuple-element.223, s32[]{:T(128)S(6)} %select_n.128, bf16[1,1024,4,4,48]{1,4,3,2,0:T(8,128)(2,1)S(1)} %get-tuple-element.222), kind=kOutput, calls=%fused_computation.3.clone.1 | convolution fusion | flops 415232000 | bytes 17582080 | tf_op jit(solution)/shard_map/while/body/eval_jaxpr/sqhd,skhd->shqk/dot_general | solution.py:41
  148.3 4.1 %fusion.71 = f32[4,1024]{1,0:T(4,128)S(1)} fusion(f32[4,1024,1024]{1,2,0:T(8,128)S(1)} %get-tuple-element.187, f32[4,1024]{1,0:T(4,128)S(1)} %get-tuple-element.188, pred[1024]{0:T(1024)(128)(4,1)S(1)} %add_compare_fusion.4), kind=kLoop, calls=%fused_computation.5.clone.1 | loop fusion | flops 16773120 | bytes 16811008 | tf_op jit(solution)/shard_map/while/body/eval_jaxpr/reduce_sum | solution.py:47
  152.4 5.6 %fusion.72 = f32[4,1,1024,4,48]{2,4,3,1,0:T(8,128)} fusion(f32[4,1,1024,4,48]{2,4,3,1,0:T(8,128)} %get-tuple-element.207, s32[]{:T(128)S(6)} %copy.89, f32[4,1024,1024]{1,2,0:T(8,128)S(1)} %get-tuple-element.187, f32[4,1024]{1,0:T(4,128)S(1)} %get-tuple-element.188, pred[1024]{0:T(1024)(128)(4,1)S(1)} %add_compare_fusion.4, ...), kind=kOutput, calls=%fused_computation.9.clone.1 | convolution fusion | flops 419430400 | bytes 17974280 | tf_op jit(solution)/shard_map/while/body/eval_jaxpr/shqk,skhd->sqhd/dot_general | solution.py:48
  158.0 0.6 bitcast_dynamic-update-slice_fusion.3
  160.9 0.7 add_compare_fusion.4
  161.5 3.3 %fusion.70 = (f32[4,1024]{1,0:T(4,128)S(1)}, f32[4,1024,1024]{1,2,0:T(8,128)S(1)}) fusion(pred[1024]{0:T(1024)(128)(4,1)S(1)} %add_compare_fusion.4, bf16[1,1024,4,4,48]{1,4,3,2,0:T(8,128)(2,1)S(1)} %get-tuple-element.223, s32[]{:T(128)S(6)} %select_n.128, bf16[1,1024,4,4,48]{1,4,3,2,0:T(8,128)(2,1)S(1)} %get-tuple-element.222), kind=kOutput, calls=%fused_computation.3.clone.1 | convolution fusion | flops 415232000 | bytes 17582080 | tf_op jit(solution)/shard_map/while/body/eval_jaxpr/sqhd,skhd->shqk/dot_general | solution.py:41
  164.9 4.1 %fusion.71 = f32[4,1024]{1,0:T(4,128)S(1)} fusion(f32[4,1024,1024]{1,2,0:T(8,128)S(1)} %get-tuple-element.187, f32[4,1024]{1,0:T(4,128)S(1)} %get-tuple-element.188, pred[1024]{0:T(1024)(128)(4,1)S(1)} %add_compare_fusion.4), kind=kLoop, calls=%fused_computation.5.clone.1 | loop fusion | flops 16773120 | bytes 16811008 | tf_op jit(solution)/shard_map/while/body/eval_jaxpr/reduce_sum | solution.py:47
  169.0 5.6 %fusion.72 = f32[4,1,1024,4,48]{2,4,3,1,0:T(8,128)} fusion(f32[4,1,1024,4,48]{2,4,3,1,0:T(8,128)} %get-tuple-element.207, s32[]{:T(128)S(6)} %copy.89, f32[4,1024,1024]{1,2,0:T(8,128)S(1)} %get-tuple-element.187, f32[4,1024]{1,0:T(4,128)S(1)} %get-tuple-element.188, pred[1024]{0:T(1024)(128)(4,1)S(1)} %add_compare_fusion.4, ...), kind=kOutput, calls=%fused_computation.9.clone.1 | convolution fusion | flops 419430400 | bytes 17974280 | tf_op jit(solution)/shard_map/while/body/eval_jaxpr/shqk,skhd->sqhd/dot_general | solution.py:48
  174.6 0.6 bitcast_dynamic-update-slice_fusion.3
  175.2 0.9 reshape.262
  176.1 0.9 reshape.268
  176.9 4.9 %broadcast_in_dim.156 = f32[64,16,16,48]{3,2,1,0:T(8,128)} broadcast(f32[64,16,48]{2,1,0:T(8,128)} %copy.51), dimensions={0,2,3} | broadcast | bytes 3342336 | tf_op jit(solution)/shard_map/jit(_where)/broadcast_in_dim | solution.py:74
  181.9 6.6 %copy.53 = f32[1024,16,48]{0,2,1:T(8,128)} copy(f32[1024,16,48]{2,1,0:T(8,128)} %bitcast.162) | data formatting | bytes 6291456 | tf_op jit(solution)/shard_map/jit(_where)/broadcast_in_dim | solution.py:74
  188.5 4.0 %fusion.32 = bf16[1024,16,48]{0,2,1:T(8,128)(2,1)S(1)} fusion(f32[1024,16,48]{0,2,1:T(8,128)} %copy.53, f32[4,1,1024,4,48]{2,4,3,1,0:T(8,128)} %get-tuple-element.52, f32[1024,16]{0,1:T(8,128)S(1)} %get-tuple-element.111, f32[1024,16]{0,1:T(8,128)S(1)} %get-tuple-element.113, f32[1024,16]{0,1:T(8,128)S(1)} %get-tuple-element.112, ...), kind=kLoop, calls=%fused_computation.37 | loop fusion | flops 5505024 | bytes 8078336 | tf_op jit(solution)/shard_map/convert_element_type | solution.py:84
  192.5 2.9 convolution_bitcast_fusion
  195.4 3.0 %copy.78 = f32[768,768]{1,0:T(8,128)} copy(f32[768,768]{0,1:T(8,128)} %convolution_bitcast_fusion) | data formatting | bytes 4718592
  198.5 7.9 %broadcast_in_dim.157 = f32[1024,768]{1,0:T(8,128)} reshape(f32[64,16,16,48]{3,2,1,0:T(8,128)} %broadcast_in_dim.156) | data formatting | bytes 6291456 | tf_op jit(solution)/shard_map/jit(_where)/broadcast_in_dim | solution.py:74
  206.5 3.6 %copy.52 = f32[1024,768]{0,1:T(8,128)} copy(f32[1024,768]{1,0:T(8,128)} %broadcast_in_dim.157) | data formatting | bytes 6291456 | tf_op jit(solution)/shard_map/jit(_where)/broadcast_in_dim | solution.py:74
  210.0 3.9 %fusion.31 = bf16[1024,768]{0,1:T(8,128)(2,1)S(1)} fusion(f32[1024,768]{0,1:T(8,128)} %copy.52, f32[4,1,1024,4,48]{2,4,3,1,0:T(8,128)} %get-tuple-element.52, f32[1024,16]{0,1:T(8,128)S(1)} %get-tuple-element.111, f32[1024,16]{0,1:T(8,128)S(1)} %get-tuple-element.113, f32[1024,16]{0,1:T(8,128)S(1)} %get-tuple-element.112, ...), kind=kLoop, calls=%fused_computation.36 | loop fusion | flops 5505024 | bytes 8078336 | tf_op jit(solution)/shard_map/convert_element_type | solution.py:84
  213.9 23.1 %reduce-scatter.4.cloned.1.call-done = f32[96,768]{1,0:T(8,128)} async-done(((f32[768,768]{1,0:T(8,128)}), f32[96,768]{1,0:T(8,128)}) %reduce-scatter.4.cloned.1.call-update) | async-done | bytes 294928
  236.9 1.8 copy.79
  238.8 4.0 %fusion.40 = bf16[1,1024,768]{2,1,0:T(8,128)(2,1)} fusion(bf16[1024,768]{0,1:T(8,128)(2,1)S(1)} %fusion.31, bf16[768,768]{1,0:T(8,128)(2,1)} %param.16), kind=kOutput, calls=%fused_computation.53 | convolution fusion | flops 1208745984 | bytes 4325376 | tf_op jit(solution)/shard_map/dot_general | solution.py:125
  242.7 39.3 %all-reduce.2.cloned.1.call-done = bf16[768,96]{1,0:T(8,128)(2,1)} async-done(((bf16[768,96]{1,0:T(8,128)(2,1)}), bf16[768,96]{1,0:T(8,128)(2,1)}) %all-reduce.2.cloned.1.call-update) | async-done | bytes 147472 | tf_op jit(solution)/shard_map/psum | solution.py:133
  282.0 1.8 copy.54
  (44 shorter events, 3.0 us)
Async XLA Ops:
  7.2 2.5 copy-start
  7.2 229.8 %reduce-scatter.4.cloned.1.call-start = ((), (), s32[]{:S(2)}) async-start(), calls=%async_computation.2 | async-start | bytes 2654208
  9.6 2.8 copy-start.11
  12.5 2.6 copy-start.12
  17.7 2.8 copy-start.2
  57.5 39.7 %copy-start.3 = (bf16[16,64,48]{1,2,0:T(8,128)(2,1)S(1)}, bf16[16,64,48]{1,2,0:T(8,128)(2,1)}, u32[]{:S(2)}) copy-start(bf16[16,64,48]{1,2,0:T(8,128)(2,1)} %copy.70) | copy-start | bytes 294916
  76.0 21.2 %copy-start.8 = (s32[512]{0:T(512)S(1)}, s32[512]{0:T(512)}, u32[]{:S(2)}) copy-start(s32[512]{0:T(512)} %iota_multiply_fusion) | copy-start | bytes 6148
  76.0 21.2 %copy-start.9 = (s32[16]{0:T(128)S(1)}, s32[16]{0:T(128)}, u32[]{:S(2)}) copy-start(s32[16]{0:T(128)} %param.12) | copy-start | bytes 196
  97.2 3.2 %copy-start.4 = (bf16[512,768]{0,1:T(8,128)(2,1)S(1)}, bf16[512,768]{0,1:T(8,128)(2,1)}, u32[]{:S(2)}) copy-start(bf16[512,768]{0,1:T(8,128)(2,1)} %copy.50) | copy-start | bytes 2359300
  99.1 1.4 copy-start.5
  181.9 6.6 %copy-start.6 = (pred[1024]{0:T(1024)(128)(4,1)S(1)}, pred[1024]{0:T(1024)(128)(4,1)}, u32[]{:S(2)}) copy-start(pred[1024]{0:T(1024)(128)(4,1)} %add_compare_fusion.2) | copy-start | bytes 3076
  188.5 4.0 %copy-start.10 = (bf16[1,1024,768]{2,1,0:T(8,128)(2,1)S(1)}, bf16[1,1024,768]{2,1,0:T(8,128)(2,1)}, u32[]{:S(2)}) copy-start(bf16[1,1024,768]{2,1,0:T(8,128)(2,1)} %param.17) | copy-start | bytes 4718596
  198.5 83.5 %all-reduce.2.cloned.1.call-start = ((), (), s32[]{:S(2)}) async-start(), calls=%async_computation.1 | async-start | bytes 393216 | tf_op jit(solution)/shard_map/psum | solution.py:133
  206.5 3.6 %copy-start.7 = (pred[1024]{0:T(1024)(128)(4,1)S(1)}, pred[1024]{0:T(1024)(128)(4,1)}, u32[]{:S(2)}) copy-start(pred[1024]{0:T(1024)(128)(4,1)} %add_compare_fusion.2) | copy-start | bytes 3076
  238.7 45.0 %copy-start.1 = (bf16[1,1024,768]{2,1,0:T(8,128)(2,1)S(1)}, bf16[1,1024,768]{2,1,0:T(8,128)(2,1)}, u32[]{:S(2)}) copy-start(bf16[1,1024,768]{2,1,0:T(8,128)(2,1)} %param.10) | copy-start | bytes 4718596
Sparse Core Ops, SparseCore 0:
  198.6 38.3 reduce-scatter.3
  240.4 41.5 all-reduce.1
where the time goes:
time: 292 us; the launch traced here: 291 us
  local copies, waits for them, and re-layouts  79 us (27%)
  waiting for transfers between devices  62.4 us (21%)
  matrix products  53.2 us (18%)
  other arithmetic  39.2 us (13%)
  blocking collectives  35 us (12%)
  between operations  14.9 us (5%)
  loops' own time  6.89 us (2%)
    psum x1, waiting for transfers between devices, body(): lax.psum(shares.astype(jnp.bfloat16), 'dp').astype(jnp.float32)  39.3 us
    unnamed x3, waiting for transfers between devices  23.1 us
    broadcast_in_dim x4, local copies, waits for them, and re-layouts, combine(): jnp.where(dilation_match[None, :, :, None], dilated_row_sum[:, None], 0.0)  23 us
    dot_general x4, matrix products, one_group(): jnp.einsum('shqk,skhd->sqhd', weights.astype(jnp.bfloat16), value_part, p...  22.5 us
    another operation x3, local copies, waits for them, and re-layouts, select_rows(): tensor.reshape(segment_height // RATE, RATE, ATTENTION_HEADS, HEAD_SIZE)  21.5 us
    all_gather x1, blocking collectives, body(): lax.all_gather(key_sel.reshape(picked, D), 'seq', axis=0, tiled=True)  18.4 us
    all_gather x1, blocking collectives, body(): lax.all_gather(value_sel.reshape(picked, D), 'seq', axis=0, tiled=True)  16.6 us
    reduce_sum x4, other arithmetic, one_group(): totals = jnp.sum(weights, axis=-1)  16.4 us
  transfers between devices with their start and end apart: 2, of which 2 were waited for; matrix products, arithmetic and copies ran while one was open for 7% of the time, Pallas kernels for 0%

commit v1 on v0

--- a/solution.py
+++ b/solution.py
@@ -130,7 +130,9 @@
         scatter_dimension=0,
         tiled=True,
     )
-    grad_part = lax.psum(shares.astype(jnp.bfloat16), "dp").astype(jnp.float32).T
+    grad_part = (
+        jnp.sum(lax.all_gather(shares.astype(jnp.bfloat16), "dp"), axis=0).astype(jnp.float32).T
+    )
     return (branch, grad_part)
 
 

time: 292 us -> 259 us (0.89)
  waiting for transfers between devices: 62.4 us -> 20.4 us
  blocking collectives: 35 us -> 46.1 us
  local copies, waits for them, and re-layouts: 79 us -> 75.7 us
    psum x1 -> x0, waiting for transfers between devices: 39.3 us -> none  [body(): lax.psum(shares.astype(jnp.bfloat16), 'dp').astype(jnp.float32)]
    unnamed x3 -> x1, waiting for transfers between devices: 23.1 us -> 0.02 us
    reduce_scatter x0 -> x1, waiting for transfers between devices: none -> 20.4 us  [body(): lax.psum_scatter(jnp.einsum('tc,td->cd', gradient_in, attn, preferred_ele...]
    all_gather x0 -> x1, blocking collectives: none -> 11.1 us  [body(): lax.all_gather(shares.astype(jnp.bfloat16), 'dp')]
    unnamed x30 -> x26, local copies, waits for them, and re-layouts: 6.73 us -> 3.18 us
  transfers between devices with their start and end apart: 2 -> 1, of which waited for: 2 -> 1; matrix products, arithmetic and copies ran while one was open for 7% -> 7% of each run, Pallas kernels for 0% -> 0%
where the time goes in v1:
time: 259 us; the launch traced here: 258 us
  local copies, waits for them, and re-layouts  75.7 us (29%)
  matrix products  51.8 us (20%)
  blocking collectives  46.1 us (18%)
  other arithmetic  40.5 us (16%)
  waiting for transfers between devices  20.4 us (8%)
  between operations  14.9 us (6%)
  loops' own time  8.39 us (3%)
    broadcast_in_dim x4, local copies, waits for them, and re-layouts, combine(): jnp.where(dilation_match[None, :, :, None], dilated_row_sum[:, None], 0.0)  23 us
    dot_general x4, matrix products, one_group(): jnp.einsum('shqk,skhd->sqhd', weights.astype(jnp.bfloat16), value_part, p...  22.5 us
    another operation x3, local copies, waits for them, and re-layouts, select_rows(): tensor.reshape(segment_height // RATE, RATE, ATTENTION_HEADS, HEAD_SIZE)  21.5 us
    reduce_scatter x1, waiting for transfers between devices, body(): lax.psum_scatter(jnp.einsum('tc,td->cd', gradient_in, attn, preferred_ele...  20.4 us
    all_gather x1, blocking collectives, body(): lax.all_gather(key_sel.reshape(picked, D), 'seq', axis=0, tiled=True)  18.4 us
    all_gather x1, blocking collectives, body(): lax.all_gather(value_sel.reshape(picked, D), 'seq', axis=0, tiled=True)  16.6 us
    reduce_sum x4, other arithmetic, one_group(): totals = jnp.sum(weights, axis=-1)  16.4 us
    dot_general x4, matrix products, one_group(): jnp.einsum('sqhd,skhd->shqk', query_part, key_part, preferred_element_typ...  13.4 us
  transfers between devices with their start and end apart: 1, of which 1 were waited for; matrix products, arithmetic and copies ran while one was open for 7% of the time, Pallas kernels for 0%

profile of v1, /device:TPU:0, one launch (start us, length us, event | category | flops | bytes accessed | tf_op | source)
XLA Modules:
  0.0 257.9 jit_solution(16686336795253595282)
XLA Ops:
  8.5 0.7 iota_compare_fusion
  9.7 2.8 %convolution_convert_fusion.3 = bf16[1024,768]{0,1:T(8,128)(2,1)S(1)} fusion(bf16[768,768]{1,0:T(8,128)(2,1)} %param.13, bf16[1,1024,768]{2,1,0:T(8,128)(2,1)S(1)} %copy-done), kind=kOutput, calls=%fused_computation.46 | convolution fusion | flops 1208745984 | bytes 4325376 | tf_op jit(solution)/shard_map/dot_general | solution.py:16
  12.5 2.6 %convolution_convert_fusion.2 = bf16[1024,768]{0,1:T(8,128)(2,1)} fusion(bf16[768,768]{1,0:T(8,128)(2,1)S(1)} %copy-done.9, bf16[1,1024,768]{2,1,0:T(8,128)(2,1)S(1)} %copy-done), kind=kOutput, calls=%fused_computation.45 | convolution fusion | flops 1208745984 | bytes 4325376 | tf_op jit(solution)/shard_map/dot_general | solution.py:16
  15.1 2.6 %convolution_convert_fusion.1 = bf16[1024,768]{0,1:T(8,128)(2,1)} fusion(bf16[768,768]{1,0:T(8,128)(2,1)S(1)} %copy-done.10, bf16[1,1024,768]{2,1,0:T(8,128)(2,1)S(1)} %copy-done), kind=kOutput, calls=%fused_computation.44 | convolution fusion | flops 1208745984 | bytes 4325376 | tf_op jit(solution)/shard_map/dot_general | solution.py:16
  17.7 2.8 %copy.59 = bf16[1024,768]{1,0:T(8,128)(2,1)} copy(bf16[1024,768]{0,1:T(8,128)(2,1)} %convolution_convert_fusion.1) | data formatting | bytes 3145728 | tf_op jit(solution)/shard_map/convert_element_type | solution.py:16
  20.4 1.6 copy.55
  22.1 1.6 copy.57
  23.6 7.2 %reshape_reshape.22 = bf16[64,16,16,48]{3,2,1,0:T(8,128)(2,1)} reshape(bf16[1024,768]{1,0:T(8,128)(2,1)} %copy.57) | data formatting | bytes 3145728 | tf_op jit(solution)/shard_map/reshape;reshape | solution.py:21
  30.8 7.2 %reshape_reshape.21 = bf16[64,16,16,48]{3,2,1,0:T(8,128)(2,1)} reshape(bf16[1024,768]{1,0:T(8,128)(2,1)} %copy.55) | data formatting | bytes 3145728 | tf_op jit(solution)/shard_map/reshape;reshape | solution.py:21
  38.0 7.2 %reshape_reshape.23 = bf16[64,16,16,48]{3,2,1,0:T(8,128)(2,1)} reshape(bf16[1024,768]{1,0:T(8,128)(2,1)} %copy.59) | data formatting | bytes 3145728 | tf_op jit(solution)/shard_map/reshape;reshape | solution.py:21
  45.2 9.0 %multiply_reduce_fusion.1 = (bf16[16,64,48]{2,0,1:T(8,128)(2,1)S(1)}, bf16[16,64,48]{2,0,1:T(8,128)(2,1)}, bf16[16,64,48]{2,0,1:T(8,128)(2,1)}) fusion(f32[16,16]{0,1:T(8,128)S(1)} %copy.90, bf16[64,16,16,48]{3,2,1,0:T(8,128)(2,1)} %reshape_reshape.22, bf16[64,16,16,48]{3,2,1,0:T(8,128)(2,1)} %reshape_reshape.23, bf16[64,16,16,48]{3,2,1,0:T(8,128)(2,1)} %reshape_reshape.21), kind=kLoop, calls=%fused_computation.25 | loop fusion | flops 6930432 | bytes 5014528
  54.1 0.9 copy.80
  55.1 1.2 reshape.266
  56.3 1.2 reshape.263
  57.5 18.4 %all_gather.12 = bf16[512,768]{1,0:T(8,128)(2,1)} all-gather(bf16[64,768]{1,0:T(8,128)(2,1)S(1)} %reshape.263), channel_id=1, replica_groups=mesh['dp'=4,'seq'=8] {'seq'}, dimensions={0}, use_global_device_ids=true | all-gather | bytes 884736 | tf_op jit(solution)/shard_map/all_gather | solution.py:104
  76.0 2.3 copy.56
  78.3 16.6 %all_gather.13 = bf16[512,768]{1,0:T(8,128)(2,1)} all-gather(bf16[64,768]{1,0:T(8,128)(2,1)S(1)} %reshape.266), channel_id=1, replica_groups=mesh['dp'=4,'seq'=8] {'seq'}, dimensions={0}, use_global_device_ids=true | all-gather | bytes 884736 | tf_op jit(solution)/shard_map/all_gather | solution.py:105
  94.9 2.3 copy.60
  97.3 1.8 bitcast_reduce_fusion
  99.1 1.4 fusion.34
  100.5 0.6 convolution_bitcast_fusion.1
  101.1 1.0 copy.61
  102.1 1.7 broadcast_in_dim.151
  103.8 1.3 broadcast_in_dim.152
  105.1 1.7 broadcast_in_dim.159
  106.8 1.3 broadcast_in_dim.160
  108.2 68.3 %while.15 = (s32[]{:T(128)}, f32[4,1,4,1024]{3,2,1,0:T(4,128)}, f32[4,1,4,1024]{3,2,1,0:T(4,128)}, f32[4,1,1024,4,48]{2,4,3,1,0:T(8,128)}, s32[4]{0:T(128)S(1)},...) while((s32[]{:T(128)}, f32[4,1,4,1024]{3,2,1,0:T(4,128)}, ...), condition=%wide.region_3.4_spmd.clone, body=%wide.region_0.3_spmd.clone.sunk | while | flops 851437568 | bytes 52434116 | solution.py:56
  108.4 0.6 dynamic_slice.41
  111.1 0.7 add_compare_fusion.4
  111.7 3.4 %fusion.70 = (f32[4,1024]{1,0:T(4,128)S(1)}, f32[4,1024,1024]{1,2,0:T(8,128)S(1)}) fusion(pred[1024]{0:T(1024)(128)(4,1)S(1)} %add_compare_fusion.4, bf16[1,1024,4,4,48]{1,4,3,2,0:T(8,128)(2,1)S(1)} %get-tuple-element.213, s32[]{:T(128)S(6)} %select_n.128, bf16[1,1024,4,4,48]{1,4,3,2,0:T(8,128)(2,1)S(1)} %get-tuple-element.212), kind=kOutput, calls=%fused_computation.3.clone.1 | convolution fusion | flops 415232000 | bytes 17582080 | tf_op jit(solution)/shard_map/while/body/eval_jaxpr/sqhd,skhd->shqk/dot_general | solution.py:41
  115.1 4.1 %fusion.71 = f32[4,1024]{1,0:T(4,128)S(1)} fusion(f32[4,1024,1024]{1,2,0:T(8,128)S(1)} %get-tuple-element.177, f32[4,1024]{1,0:T(4,128)S(1)} %get-tuple-element.178, pred[1024]{0:T(1024)(128)(4,1)S(1)} %add_compare_fusion.4), kind=kLoop, calls=%fused_computation.5.clone.1 | loop fusion | flops 16773120 | bytes 16811008 | tf_op jit(solution)/shard_map/while/body/eval_jaxpr/reduce_sum | solution.py:47
  119.2 5.7 %fusion.72 = f32[4,1,1024,4,48]{2,4,3,1,0:T(8,128)} fusion(f32[4,1,1024,4,48]{2,4,3,1,0:T(8,128)} %get-tuple-element.197, s32[]{:T(128)S(6)} %copy.99, f32[4,1024,1024]{1,2,0:T(8,128)S(1)} %get-tuple-element.177, f32[4,1024]{1,0:T(4,128)S(1)} %get-tuple-element.178, pred[1024]{0:T(1024)(128)(4,1)S(1)} %add_compare_fusion.4, ...), kind=kOutput, calls=%fused_computation.9.clone.1 | convolution fusion | flops 419430400 | bytes 17974280 | tf_op jit(solution)/shard_map/while/body/eval_jaxpr/shqk,skhd->sqhd/dot_general | solution.py:48
  125.4 0.6 dynamic_slice.41
  128.1 0.7 add_compare_fusion.4
  128.8 3.4 %fusion.70 = (f32[4,1024]{1,0:T(4,128)S(1)}, f32[4,1024,1024]{1,2,0:T(8,128)S(1)}) fusion(pred[1024]{0:T(1024)(128)(4,1)S(1)} %add_compare_fusion.4, bf16[1,1024,4,4,48]{1,4,3,2,0:T(8,128)(2,1)S(1)} %get-tuple-element.213, s32[]{:T(128)S(6)} %select_n.128, bf16[1,1024,4,4,48]{1,4,3,2,0:T(8,128)(2,1)S(1)} %get-tuple-element.212), kind=kOutput, calls=%fused_computation.3.clone.1 | convolution fusion | flops 415232000 | bytes 17582080 | tf_op jit(solution)/shard_map/while/body/eval_jaxpr/sqhd,skhd->shqk/dot_general | solution.py:41
  132.1 4.1 %fusion.71 = f32[4,1024]{1,0:T(4,128)S(1)} fusion(f32[4,1024,1024]{1,2,0:T(8,128)S(1)} %get-tuple-element.177, f32[4,1024]{1,0:T(4,128)S(1)} %get-tuple-element.178, pred[1024]{0:T(1024)(128)(4,1)S(1)} %add_compare_fusion.4), kind=kLoop, calls=%fused_computation.5.clone.1 | loop fusion | flops 16773120 | bytes 16811008 | tf_op jit(solution)/shard_map/while/body/eval_jaxpr/reduce_sum | solution.py:47
  136.2 5.6 %fusion.72 = f32[4,1,1024,4,48]{2,4,3,1,0:T(8,128)} fusion(f32[4,1,1024,4,48]{2,4,3,1,0:T(8,128)} %get-tuple-element.197, s32[]{:T(128)S(6)} %copy.99, f32[4,1024,1024]{1,2,0:T(8,128)S(1)} %get-tuple-element.177, f32[4,1024]{1,0:T(4,128)S(1)} %get-tuple-element.178, pred[1024]{0:T(1024)(128)(4,1)S(1)} %add_compare_fusion.4, ...), kind=kOutput, calls=%fused_computation.9.clone.1 | convolution fusion | flops 419430400 | bytes 17974280 | tf_op jit(solution)/shard_map/while/body/eval_jaxpr/shqk,skhd->sqhd/dot_general | solution.py:48
  142.4 0.6 dynamic_slice.41
  145.1 0.7 add_compare_fusion.4
  145.8 3.3 %fusion.70 = (f32[4,1024]{1,0:T(4,128)S(1)}, f32[4,1024,1024]{1,2,0:T(8,128)S(1)}) fusion(pred[1024]{0:T(1024)(128)(4,1)S(1)} %add_compare_fusion.4, bf16[1,1024,4,4,48]{1,4,3,2,0:T(8,128)(2,1)S(1)} %get-tuple-element.213, s32[]{:T(128)S(6)} %select_n.128, bf16[1,1024,4,4,48]{1,4,3,2,0:T(8,128)(2,1)S(1)} %get-tuple-element.212), kind=kOutput, calls=%fused_computation.3.clone.1 | convolution fusion | flops 415232000 | bytes 17582080 | tf_op jit(solution)/shard_map/while/body/eval_jaxpr/sqhd,skhd->shqk/dot_general | solution.py:41
  149.1 4.1 %fusion.71 = f32[4,1024]{1,0:T(4,128)S(1)} fusion(f32[4,1024,1024]{1,2,0:T(8,128)S(1)} %get-tuple-element.177, f32[4,1024]{1,0:T(4,128)S(1)} %get-tuple-element.178, pred[1024]{0:T(1024)(128)(4,1)S(1)} %add_compare_fusion.4), kind=kLoop, calls=%fused_computation.5.clone.1 | loop fusion | flops 16773120 | bytes 16811008 | tf_op jit(solution)/shard_map/while/body/eval_jaxpr/reduce_sum | solution.py:47
  153.2 5.6 %fusion.72 = f32[4,1,1024,4,48]{2,4,3,1,0:T(8,128)} fusion(f32[4,1,1024,4,48]{2,4,3,1,0:T(8,128)} %get-tuple-element.197, s32[]{:T(128)S(6)} %copy.99, f32[4,1024,1024]{1,2,0:T(8,128)S(1)} %get-tuple-element.177, f32[4,1024]{1,0:T(4,128)S(1)} %get-tuple-element.178, pred[1024]{0:T(1024)(128)(4,1)S(1)} %add_compare_fusion.4, ...), kind=kOutput, calls=%fused_computation.9.clone.1 | convolution fusion | flops 419430400 | bytes 17974280 | tf_op jit(solution)/shard_map/while/body/eval_jaxpr/shqk,skhd->sqhd/dot_general | solution.py:48
  158.8 0.6 bitcast_dynamic-update-slice_fusion.3
  159.4 0.6 dynamic_slice.41
  162.1 0.7 add_compare_fusion.4
  162.8 3.3 %fusion.70 = (f32[4,1024]{1,0:T(4,128)S(1)}, f32[4,1024,1024]{1,2,0:T(8,128)S(1)}) fusion(pred[1024]{0:T(1024)(128)(4,1)S(1)} %add_compare_fusion.4, bf16[1,1024,4,4,48]{1,4,3,2,0:T(8,128)(2,1)S(1)} %get-tuple-element.213, s32[]{:T(128)S(6)} %select_n.128, bf16[1,1024,4,4,48]{1,4,3,2,0:T(8,128)(2,1)S(1)} %get-tuple-element.212), kind=kOutput, calls=%fused_computation.3.clone.1 | convolution fusion | flops 415232000 | bytes 17582080 | tf_op jit(solution)/shard_map/while/body/eval_jaxpr/sqhd,skhd->shqk/dot_general | solution.py:41
  166.1 4.1 %fusion.71 = f32[4,1024]{1,0:T(4,128)S(1)} fusion(f32[4,1024,1024]{1,2,0:T(8,128)S(1)} %get-tuple-element.177, f32[4,1024]{1,0:T(4,128)S(1)} %get-tuple-element.178, pred[1024]{0:T(1024)(128)(4,1)S(1)} %add_compare_fusion.4), kind=kLoop, calls=%fused_computation.5.clone.1 | loop fusion | flops 16773120 | bytes 16811008 | tf_op jit(solution)/shard_map/while/body/eval_jaxpr/reduce_sum | solution.py:47
  170.2 5.6 %fusion.72 = f32[4,1,1024,4,48]{2,4,3,1,0:T(8,128)} fusion(f32[4,1,1024,4,48]{2,4,3,1,0:T(8,128)} %get-tuple-element.197, s32[]{:T(128)S(6)} %copy.99, f32[4,1024,1024]{1,2,0:T(8,128)S(1)} %get-tuple-element.177, f32[4,1024]{1,0:T(4,128)S(1)} %get-tuple-element.178, pred[1024]{0:T(1024)(128)(4,1)S(1)} %add_compare_fusion.4, ...), kind=kOutput, calls=%fused_computation.9.clone.1 | convolution fusion | flops 419430400 | bytes 17974280 | tf_op jit(solution)/shard_map/while/body/eval_jaxpr/shqk,skhd->sqhd/dot_general | solution.py:48
  175.9 0.6 bitcast_dynamic-update-slice_fusion.3
  176.5 0.9 reshape.262
  177.3 0.9 reshape.268
  178.2 4.9 %broadcast_in_dim.156 = f32[64,16,16,48]{3,2,1,0:T(8,128)} broadcast(f32[64,16,48]{2,1,0:T(8,128)} %copy.61), dimensions={0,2,3} | broadcast | bytes 3342336 | tf_op jit(solution)/shard_map/jit(_where)/broadcast_in_dim | solution.py:74
  183.1 6.5 %copy.63 = f32[1024,16,48]{0,2,1:T(8,128)} copy(f32[1024,16,48]{2,1,0:T(8,128)} %bitcast.162) | data formatting | bytes 6291456 | tf_op jit(solution)/shard_map/jit(_where)/broadcast_in_dim | solution.py:74
  189.7 4.0 %fusion.32 = bf16[1024,16,48]{0,2,1:T(8,128)(2,1)S(1)} fusion(f32[1024,16,48]{0,2,1:T(8,128)} %copy.63, f32[4,1,1024,4,48]{2,4,3,1,0:T(8,128)} %get-tuple-element.52, f32[1024,16]{0,1:T(8,128)S(1)} %get-tuple-element.101, f32[1024,16]{0,1:T(8,128)S(1)} %get-tuple-element.103, f32[1024,16]{0,1:T(8,128)S(1)} %get-tuple-element.102, ...), kind=kLoop, calls=%fused_computation.37 | loop fusion | flops 5505024 | bytes 8078336 | tf_op jit(solution)/shard_map/convert_element_type | solution.py:84
  193.8 2.9 %convolution_bitcast_fusion = f32[768,768]{0,1:T(8,128)} fusion(bf16[1024,768]{0,1:T(8,128)(2,1)S(1)} %bitcast.168, bf16[1,1024,768]{2,1,0:T(8,128)(2,1)S(1)} %copy-done.8), kind=kOutput, calls=%fused_computation.42 | convolution fusion | flops 1207959552 | bytes 5505024 | tf_op jit(solution)/shard_map/tc,td->cd/dot_general | solution.py:128
  196.6 3.0 %copy.88 = f32[768,768]{1,0:T(8,128)} copy(f32[768,768]{0,1:T(8,128)} %convolution_bitcast_fusion) | data formatting | bytes 4718592
  199.7 7.9 %broadcast_in_dim.157 = f32[1024,768]{1,0:T(8,128)} reshape(f32[64,16,16,48]{3,2,1,0:T(8,128)} %broadcast_in_dim.156) | data formatting | bytes 6291456 | tf_op jit(solution)/shard_map/jit(_where)/broadcast_in_dim | solution.py:74
  207.6 3.5 %copy.62 = f32[1024,768]{0,1:T(8,128)} copy(f32[1024,768]{1,0:T(8,128)} %broadcast_in_dim.157) | data formatting | bytes 6291456 | tf_op jit(solution)/shard_map/jit(_where)/broadcast_in_dim | solution.py:74
  211.2 3.9 %fusion.31 = bf16[1024,768]{0,1:T(8,128)(2,1)S(1)} fusion(f32[1024,768]{0,1:T(8,128)} %copy.62, f32[4,1,1024,4,48]{2,4,3,1,0:T(8,128)} %get-tuple-element.52, f32[1024,16]{0,1:T(8,128)S(1)} %get-tuple-element.101, f32[1024,16]{0,1:T(8,128)S(1)} %get-tuple-element.103, f32[1024,16]{0,1:T(8,128)S(1)} %get-tuple-element.102, ...), kind=kLoop, calls=%fused_computation.36 | loop fusion | flops 5505024 | bytes 8078336 | tf_op jit(solution)/shard_map/convert_element_type | solution.py:84
  215.2 2.6 %fusion.40 = bf16[1,1024,768]{2,1,0:T(8,128)(2,1)} fusion(bf16[1024,768]{0,1:T(8,128)(2,1)S(1)} %fusion.31, bf16[768,768]{1,0:T(8,128)(2,1)S(1)} %copy-done.11), kind=kOutput, calls=%fused_computation.53 | convolution fusion | flops 1208745984 | bytes 4325376 | tf_op jit(solution)/shard_map/dot_general | solution.py:125
  217.8 20.4 %reduce-scatter.4.cloned.1.call-done = f32[96,768]{1,0:T(8,128)} async-done(((f32[768,768]{1,0:T(8,128)}), f32[96,768]{1,0:T(8,128)}) %reduce-scatter.4.cloned.1.call-update) | async-done | bytes 294928 | tf_op jit(solution)/shard_map/reduce_scatter | solution.py:127
  238.2 1.0 convert_element_type.80
  239.1 11.1 %all-gather = bf16[384,768]{1,0:T(8,128)(2,1)S(1)} all-gather(bf16[96,768]{1,0:T(8,128)(2,1)S(1)} %convert_element_type.80), channel_id=2, replica_groups=mesh['dp'=4,'seq'=8] {'dp'}, dimensions={0}, use_global_device_ids=true | all-gather | bytes 737280 | tf_op jit(solution)/shard_map/all_gather | solution.py:134
  250.3 0.7 convert_bitcast_fusion
  (41 shorter events, 2.6 us)
Async XLA Ops:
  7.2 2.5 copy-start
  7.2 231.0 %reduce-scatter.4.cloned.1.call-start = ((), (), s32[]{:S(2)}) async-start(), calls=%async_computation.1 | async-start | bytes 2654208 | tf_op jit(solution)/shard_map/reduce_scatter | solution.py:127
  9.6 2.8 %copy-start.9 = (bf16[768,768]{1,0:T(8,128)(2,1)S(1)}, bf16[768,768]{1,0:T(8,128)(2,1)}, u32[]{:S(2)}) copy-start(bf16[768,768]{1,0:T(8,128)(2,1)} %param.14) | copy-start | bytes 3538948
  12.5 2.6 %copy-start.10 = (bf16[768,768]{1,0:T(8,128)(2,1)S(1)}, bf16[768,768]{1,0:T(8,128)(2,1)}, u32[]{:S(2)}) copy-start(bf16[768,768]{1,0:T(8,128)(2,1)} %param.15) | copy-start | bytes 3538948
  17.7 2.8 %copy-start.2 = (bf16[1024,768]{0,1:T(8,128)(2,1)S(1)}, bf16[1024,768]{0,1:T(8,128)(2,1)}, u32[]{:S(2)}) copy-start(bf16[1024,768]{0,1:T(8,128)(2,1)} %convolution_convert_fusion.2) | copy-start | bytes 4718596
  57.5 39.7 %copy-start.3 = (bf16[16,64,48]{1,2,0:T(8,128)(2,1)S(1)}, bf16[16,64,48]{1,2,0:T(8,128)(2,1)}, u32[]{:S(2)}) copy-start(bf16[16,64,48]{1,2,0:T(8,128)(2,1)} %copy.80) | copy-start | bytes 294916
  76.0 21.2 %copy-start.6 = (s32[512]{0:T(512)S(1)}, s32[512]{0:T(512)}, u32[]{:S(2)}) copy-start(s32[512]{0:T(512)} %iota_multiply_fusion) | copy-start | bytes 6148
  76.0 21.2 %copy-start.7 = (s32[16]{0:T(128)S(1)}, s32[16]{0:T(128)}, u32[]{:S(2)}) copy-start(s32[16]{0:T(128)} %param.12) | copy-start | bytes 196
  97.2 3.2 %copy-start.4 = (bf16[512,768]{0,1:T(8,128)(2,1)S(1)}, bf16[512,768]{0,1:T(8,128)(2,1)}, u32[]{:S(2)}) copy-start(bf16[512,768]{0,1:T(8,128)(2,1)} %copy.60) | copy-start | bytes 2359300
  99.1 1.4 copy-start.5
  189.7 4.0 %copy-start.8 = (bf16[1,1024,768]{2,1,0:T(8,128)(2,1)S(1)}, bf16[1,1024,768]{2,1,0:T(8,128)(2,1)}, u32[]{:S(2)}) copy-start(bf16[1,1024,768]{2,1,0:T(8,128)(2,1)} %param.17) | copy-start | bytes 4718596
  211.2 4.0 %copy-start.11 = (bf16[768,768]{1,0:T(8,128)(2,1)S(1)}, bf16[768,768]{1,0:T(8,128)(2,1)}, u32[]{:S(2)}) copy-start(bf16[768,768]{1,0:T(8,128)(2,1)} %param.16) | copy-start | bytes 3538948
  215.1 35.9 %copy-start.1 = (bf16[1,1024,768]{2,1,0:T(8,128)(2,1)S(1)}, bf16[1,1024,768]{2,1,0:T(8,128)(2,1)}, u32[]{:S(2)}) copy-start(bf16[1,1024,768]{2,1,0:T(8,128)(2,1)} %param.10) | copy-start | bytes 4718596
Sparse Core Ops, SparseCore 0:
  199.8 38.3 reduce-scatter.3
